TPU v7x, 128 devices: a whole 4x4x4 slice. The times are simulated.
128 devices in a mesh: replica: 32 (over z, y, core), shard: 4 (over x).
Axes of the slice: x: 4, y: 4, z: 4, core: 2. Of those that a mesh axis runs over, the one named last changes fastest.
Arguments:
- acts: bfloat16 [2, 65536, 1280], P(None, 'replica', 'shard'), may hold values from -6 to 6
- cots: bfloat16 [2, 65536, 1280], P(None, 'replica'), may hold values from -6 to 6
- errors: float32 [32, 2, 1280, 1280], P('replica', None, 'shard'), may hold values from -4 to 4
- weights: float32 [2, 1280, 1280], P(None, 'shard'), may hold values from -0.3 to 0.3
- momentum: float32 [2, 1280, 1280], P(None, 'shard'), may hold values from -3 to 3
- start_q: float32 [2, 1280, 32], replicated, may hold values from -6 to 6
- vec_grads: float32 [32, 4, 1280], P('replica', None, 'shard'), may hold values from -6 to 6
- vec_weights: float32 [4, 1280], P(None, 'shard'), may hold values from 0.5 to 1.5
- vec_momentum: float32 [4, 1280], P(None, 'shard'), may hold values from -6 to 6
Outputs:
- new_errors: float32 [32, 2, 1280, 1280], P('replica', None, 'shard')
- new_weights: float32 [2, 1280, 1280], P(None, 'shard')
- new_momentum: float32 [2, 1280, 1280], P(None, 'shard')
- new_vec_weights: float32 [4, 1280], P(None, 'shard')
- new_vec_momentum: float32 [4, 1280], P(None, 'shard')
All inputs are finite; a program needn't handle non-finite values.
Results may differ from a plain program's by a relative error of at most 0.0003.
Values sent between devices are 32-bit elements; how exact they have to be, the bound alone decides.
No kernel may reach another device: no remote copies, remote signals or barrier semaphores. Data moves between devices by JAX's collectives and lax.ppermute only.
A program may use at most 128 MiB of HBM per device.

v0:
```python
import math
import jax
import jax.numpy as jnp
from jax import lax
from jax.sharding import PartitionSpec as P

HIGH = lax.Precision.HIGHEST


def finish(block, gram):
    lower = jnp.linalg.cholesky(gram)
    return lax.linalg.triangular_solve(lower, block, left_side=False, lower=True, transpose_a=True)


def orth_local(block):
    gram = jnp.einsum("mdk,mdl->mkl", block, block, precision=HIGH)
    return finish(block, gram)


def orth_rows(block):
    gram = jnp.einsum("mdk,mdl->mkl", block, block, precision=HIGH)
    gram = lax.psum(gram, "shard")
    return finish(block, gram)


def project_rows(full, right):
    return jnp.einsum("mde,mek->mdk", full, right, precision=HIGH)


def reduce_right(full, left):
    terms = jnp.einsum("mde,mdk->mek", full, left, precision=HIGH)
    return lax.psum(terms, ("replica", "shard"))


def body(acts, cots, errors, weights, momentum, start_q, vec_grads, vec_weights, vec_momentum):
    tok_rows = acts.shape[1]
    replicas = float(lax.axis_size("replica"))
    grads = jnp.einsum("mtd,mte->mde", acts, cots, preferred_element_type=jnp.float32)
    full = grads * (1.0 / math.sqrt(tok_rows)) + errors[0]
    local_left = project_rows(full, start_q)
    vec_total = lax.psum(vec_grads[0], "replica")
    left_sum = lax.psum(local_left, "replica")
    left = orth_rows(left_sum)
    right = reduce_right(full, left)
    right_hat = orth_local(right)
    left_sum = lax.psum(project_rows(full, right_hat), "replica")
    left = orth_rows(left_sum)
    right = reduce_right(full, left)
    approx = jnp.einsum("mdk,mek->mde", left, right, precision=HIGH) / replicas
    new_errors = (full - approx)[None]
    new_momentum = 0.9 * momentum + approx
    new_weights = weights - 0.1 * new_momentum
    vec_moved = 0.9 * vec_momentum + vec_total / replicas
    return (new_errors, new_weights, new_momentum, vec_weights - 0.1 * vec_moved, vec_moved)


def solution(mesh):
    placed = (
        P(None, "replica", "shard"),
        P(None, "replica", None),
        P("replica", None, "shard", None),
        P(None, "shard", None),
        P(None, "shard", None),
        P(),
        P("replica", None, "shard"),
        P(None, "shard"),
        P(None, "shard"),
    )
    return jax.shard_map(
        body,
        mesh=mesh,
        in_specs=placed,
        out_specs=(
            P("replica", None, "shard", None),
            P(None, "shard", None),
            P(None, "shard", None),
            P(None, "shard"),
            P(None, "shard"),
        ),
        check_vma=False,
    )
```

profile of v0, /device:TPU:1, one launch (start us, length us, event | category | flops | bytes accessed | tf_op | source)
XLA Modules:
  0.0 609.8 jit_solution(3013208280082749145)
XLA Ops:
  7.2 1.7 copy-done
  8.9 8.5 %fusion = f32[2,320,1280]{2,1,0:T(8,128)S(1)} fusion(bf16[2,2048,320]{1,2,0:T(8,128)(2,1)S(1)} %copy-done, bf16[2,2048,1280]{2,1,0:T(8,128)(2,1)} %param.13, f32[1,2,320,1280]{3,2,1,0:T(8,128)} %param.14), kind=kOutput, calls=%fused_computation.2 | convolution fusion | flops 3357081600 | bytes 19660800 | tf_op jit(solution)/shard_map/mtd,mte->mde/dot_general | solution.py:38
  17.4 1.7 copy-done.1
  19.1 3.5 fusion.9
  22.7 101.0 %all-reduce.5.cloned.1.call-done = f32[2,320,32]{1,2,0:T(8,128)} async-done(((f32[2,320,32]{1,2,0:T(8,128)}), f32[2,320,32]{1,2,0:T(8,128)}) %all-reduce.5.cloned.1.call-update) | async-done | bytes 81936 | tf_op jit(solution)/shard_map/psum | solution.py:42
  123.7 1.2 fusion.10
  124.9 13.2 %psum.50 = f32[2,32,32]{1,2,0:T(8,128)S(1)} all-reduce(f32[2,32,32]{1,2,0:T(8,128)S(1)} %fusion.10), channel_id=1, replica_groups=mesh['replica'=32,'shard'=4] {'shard'}, use_global_device_ids=true, to_apply=%region_1.0 | all-reduce | flops 2048 | bytes 16384 | tf_op jit(solution)/shard_map/psum | solution.py:22
  138.2 5.9 custom-call.13
  144.1 0.1 compare_reduce_fusion.2
  144.3 4.9 custom-call.14
  149.3 1.2 convolution_bitcast_fusion.1
  150.5 4.6 fusion.11
  155.1 0.2 all-reduce.9.cloned.1.call-start
  155.4 144.9 %all-reduce.7.cloned.1.call-done = f32[2,1280,32]{1,2,0:T(8,128)} async-done(((f32[2,1280,32]{1,2,0:T(8,128)}), f32[2,1280,32]{1,2,0:T(8,128)}) %all-reduce.7.cloned.1.call-update) | async-done | bytes 327696 | tf_op jit(solution)/shard_map/psum | solution.py:32
  300.3 1.5 fusion.12
  301.9 5.9 custom-call.15
  307.8 0.1 compare_reduce_fusion.1
  308.0 4.9 custom-call.9
  312.9 1.5 fusion.3
  314.4 5.4 fusion.13
  319.9 62.7 %psum.55 = f32[4,320]{1,0:T(4,128)S(1)} all-reduce(f32[4,320]{1,0:T(4,128)S(1)} %bitcast.57), channel_id=1, replica_groups=mesh['replica'=32,'shard'=4] {'replica'}, use_global_device_ids=true, to_apply=%region_8.11 | all-reduce | flops 1280 | bytes 10240 | tf_op jit(solution)/shard_map/psum | solution.py:41
  382.6 32.9 %all-reduce.9.cloned.1.call-done = f32[2,320,32]{1,2,0:T(8,128)} async-done(((f32[2,320,32]{1,2,0:T(8,128)}), f32[2,320,32]{1,2,0:T(8,128)}) %all-reduce.9.cloned.1.call-update) | async-done | bytes 81936 | tf_op jit(solution)/shard_map/psum | solution.py:46
  415.5 1.2 fusion.14
  416.7 13.2 %psum.53 = f32[2,32,32]{1,2,0:T(8,128)S(1)} all-reduce(f32[2,32,32]{1,2,0:T(8,128)S(1)} %fusion.14), channel_id=1, replica_groups=mesh['replica'=32,'shard'=4] {'shard'}, use_global_device_ids=true, to_apply=%region_6.9 | all-reduce | flops 2048 | bytes 16384 | tf_op jit(solution)/shard_map/psum | solution.py:22
  430.1 5.9 custom-call.16
  436.0 0.1 compare_reduce_fusion
  436.2 4.9 custom-call.17
  441.1 1.2 convolution_bitcast_fusion
  442.3 4.6 fusion.15
  447.0 0.6 multiply_subtract_fusion.1
  447.6 144.5 %all-reduce.11.cloned.1.call-done = f32[2,1280,32]{1,2,0:T(8,128)} async-done(((f32[2,1280,32]{1,2,0:T(8,128)}), f32[2,1280,32]{1,2,0:T(8,128)}) %all-reduce.11.cloned.1.call-update) | async-done | bytes 327696 | tf_op jit(solution)/shard_map/psum | solution.py:32
  592.0 11.3 %multiply_subtract_fusion = (f32[2,320,1280]{2,1,0:T(8,128)}, f32[2,320,1280]{2,1,0:T(8,128)}, f32[1,2,320,1280]{3,2,1,0:T(8,128)}) fusion(f32[2,320,1280]{2,1,0:T(8,128)} %param.15, f32[2,320,1280]{2,1,0:T(8,128)} %param.16, f32[2,320,1280]{2,1,0:T(8,128)} %copy-done.1, f32[2,320,32]{1,2,0:T(8,128)S(1)} %convolution_bitcast_fusion, ...), kind=kOutput, calls=%fused_computation.3 | convolution fusion | flops 319488000 | bytes 20070400 | tf_op jit(solution)/shard_map/mdk,mek->mde/dot_general | solution.py:49
  (31 shorter events, 0.8 us)
Async XLA Ops:
  7.2 1.7 copy-start
  7.2 11.9 %copy-start.2 = (f32[2,1280,32]{1,2,0:T(8,128)S(1)}, f32[2,1280,32]{1,2,0:T(8,128)}, u32[]{:S(2)}) copy-start(f32[2,1280,32]{1,2,0:T(8,128)} %param.17) | copy-start | bytes 983044
  7.2 116.5 %all-reduce.5.cloned.1.call-start = ((), (), s32[]{:S(2)}) async-start(), calls=%async_computation | async-start | bytes 196608 | tf_op jit(solution)/shard_map/psum | solution.py:42
  17.4 1.7 copy-start.1
  22.7 277.6 %all-reduce.7.cloned.1.call-start = ((), (), s32[]{:S(2)}) async-start(), calls=%async_computation.1 | async-start | bytes 655360 | tf_op jit(solution)/shard_map/psum | solution.py:32
  155.1 164.8 %copy-start.3 = (f32[1,4,320]{2,1,0:T(4,128)S(1)}, f32[1,4,320]{2,1,0:T(4,128)}, u32[]{:S(2)}) copy-start(f32[1,4,320]{2,1,0:T(4,128)} %param.18) | copy-start | bytes 15364
  155.1 260.4 %all-reduce.9.cloned.1.call-start = ((), (), s32[]{:S(2)}) async-start(), calls=%async_computation.2 | async-start | bytes 196608 | tf_op jit(solution)/shard_map/psum | solution.py:46
  319.8 127.1 %copy-start.4 = (f32[4,320]{1,0:T(4,128)S(1)}, f32[4,320]{1,0:T(4,128)}, u32[]{:S(2)}) copy-start(f32[4,320]{1,0:T(4,128)} %param.19) | copy-start | bytes 15364
  319.8 127.2 %copy-start.5 = (f32[4,320]{1,0:T(4,128)S(1)}, f32[4,320]{1,0:T(4,128)}, u32[]{:S(2)}) copy-start(f32[4,320]{1,0:T(4,128)} %param.20) | copy-start | bytes 15364
  319.8 272.2 %all-reduce.11.cloned.1.call-start = ((), (), s32[]{:S(2)}) async-start(), calls=%async_computation.3 | async-start | bytes 655360 | tf_op jit(solution)/shard_map/psum | solution.py:32
Sparse Core Ops, SparseCore 0:
  22.8 100.8 all-reduce.4
  155.2 144.9 all-reduce.6
  319.9 95.5 all-reduce.8
  447.1 144.9 all-reduce.10
where the time goes:
time: 610 us
  waiting for transfers between devices  423 us (69%)
  blocking collectives  89.2 us (15%)
  matrix products  45.7 us (7%)
  other arithmetic  33.7 us (6%)
  between operations  13.9 us (2%)
    psum x2, waiting for transfers between devices, reduce_right(): return lax.psum(terms, ('replica', 'shard'))  289 us
    psum x1, waiting for transfers between devices, body(): left_sum = lax.psum(local_left, 'replica')  101 us
    psum x1, blocking collectives, body(): vec_total = lax.psum(vec_grads[0], 'replica')  62.7 us
    psum x1, waiting for transfers between devices, body(): left_sum = lax.psum(project_rows(full, right_hat), 'replica')  32.9 us
    psum x2, blocking collectives, orth_rows(): gram = lax.psum(gram, 'shard')  26.5 us
    another operation x10, other arithmetic, finish(): lower = jnp.linalg.cholesky(gram)  18.1 us
    another operation x7, other arithmetic, finish(): lax.linalg.triangular_solve(lower, block, left_side=False, lower=True, tr...  15 us
  transfers between devices with their start and end apart: 4, of which 4 were waited for; matrix products, arithmetic and copies ran while one was open for 0% of the time, Pallas kernels for 0%

commit v1 on v0

--- a/solution.py
+++ b/solution.py
@@ -29,7 +29,7 @@
 
 def reduce_right(full, left):
     terms = jnp.einsum("mde,mdk->mek", full, left, precision=HIGH)
-    return lax.psum(terms, ("replica", "shard"))
+    return lax.psum(lax.psum(terms, "shard"), "replica")
 
 
 def body(acts, cots, errors, weights, momentum, start_q, vec_grads, vec_weights, vec_momentum):

time: 610 us -> 636 us (1.043)
  waiting for transfers between devices: 423 us -> 444 us
    psum x1, waiting for transfers between devices: 32.9 us -> 96.9 us  [body(): left_sum = lax.psum(project_rows(full, right_hat), 'replica')]
    psum x2 -> x4, waiting for transfers between devices: 289 us -> 246 us  [reduce_right(): return lax.psum(lax.psum(terms, 'shard'), 'replica')]
  transfers between devices with their start and end apart: 4 -> 6, of which waited for: 4 -> 5; matrix products, arithmetic and copies ran while one was open for 0% -> 0% of each run, Pallas kernels for 0% -> 0%
where the time goes in v1:
time: 636 us
  waiting for transfers between devices  444 us (70%)
  blocking collectives  94.6 us (15%)
  matrix products  45.7 us (7%)
  other arithmetic  33.7 us (5%)
  between operations  14.3 us (2%)
    psum x4, waiting for transfers between devices, reduce_right(): return lax.psum(lax.psum(terms, 'shard'), 'replica')  246 us
    psum x1, waiting for transfers between devices, body(): left_sum = lax.psum(local_left, 'replica')  101 us
    psum x1, waiting for transfers between devices, body(): left_sum = lax.psum(project_rows(full, right_hat), 'replica')  96.9 us
    psum x1, blocking collectives, body(): vec_total = lax.psum(vec_grads[0], 'replica')  68.1 us
    psum x2, blocking collectives, orth_rows(): gram = lax.psum(gram, 'shard')  26.5 us
    another operation x10, other arithmetic, finish(): lower = jnp.linalg.cholesky(gram)  18.1 us
    another operation x7, other arithmetic, finish(): lax.linalg.triangular_solve(lower, block, left_side=False, lower=True, tr...  15 us
  transfers between devices with their start and end apart: 6, of which 5 were waited for; matrix products, arithmetic and copies ran while one was open for 0% of the time, Pallas kernels for 0%

profile of v1, /device:TPU:1, one launch (start us, length us, event | category | flops | bytes accessed | tf_op | source)
XLA Modules:
  0.0 635.9 jit_solution(4426941605878629004)
XLA Ops:
  7.2 1.7 copy-done
  8.9 8.5 %fusion = f32[2,320,1280]{2,1,0:T(8,128)S(1)} fusion(bf16[2,2048,320]{1,2,0:T(8,128)(2,1)S(1)} %copy-done, bf16[2,2048,1280]{2,1,0:T(8,128)(2,1)} %param.13, f32[1,2,320,1280]{3,2,1,0:T(8,128)} %param.14), kind=kOutput, calls=%fused_computation.2 | convolution fusion | flops 3357081600 | bytes 19660800 | tf_op jit(solution)/shard_map/mtd,mte->mde/dot_general | solution.py:38
  17.4 1.7 copy-done.1
  19.1 3.5 fusion.9
  22.7 101.0 %all-reduce.7.cloned.1.call-done = f32[2,320,32]{1,2,0:T(8,128)} async-done(((f32[2,320,32]{1,2,0:T(8,128)}), f32[2,320,32]{1,2,0:T(8,128)}) %all-reduce.7.cloned.1.call-update) | async-done | bytes 81936 | tf_op jit(solution)/shard_map/psum | solution.py:42
  123.7 1.2 fusion.10
  124.9 13.2 %psum.64 = f32[2,32,32]{1,2,0:T(8,128)S(1)} all-reduce(f32[2,32,32]{1,2,0:T(8,128)S(1)} %fusion.10), channel_id=1, replica_groups=mesh['replica'=32,'shard'=4] {'shard'}, use_global_device_ids=true, to_apply=%region_1.0 | all-reduce | flops 2048 | bytes 16384 | tf_op jit(solution)/shard_map/psum | solution.py:22
  138.2 5.9 custom-call.13
  144.1 0.1 compare_reduce_fusion.2
  144.3 4.9 custom-call.14
  149.3 1.2 convolution_bitcast_fusion.1
  150.5 4.6 fusion.11
  155.2 41.4 %all-reduce.9.cloned.1.call-done = f32[2,1280,32]{1,2,0:T(8,128)} async-done(((f32[2,1280,32]{1,2,0:T(8,128)}), f32[2,1280,32]{1,2,0:T(8,128)}) %all-reduce.9.cloned.1.call-update) | async-done | bytes 327696 | tf_op jit(solution)/shard_map/psum | solution.py:32
  196.6 0.2 all-reduce.13.cloned.1.call-start
  196.8 108.0 %all-reduce.11.cloned.1.call-done = f32[2,1280,32]{1,2,0:T(8,128)} async-done(((f32[2,1280,32]{1,2,0:T(8,128)}), f32[2,1280,32]{1,2,0:T(8,128)}) %all-reduce.11.cloned.1.call-update) | async-done | bytes 327696 | tf_op jit(solution)/shard_map/psum | solution.py:32
  304.8 1.5 fusion.12
  306.4 5.9 custom-call.15
  312.3 0.1 compare_reduce_fusion.1
  312.5 4.9 custom-call.9
  317.4 1.5 fusion.3
  318.9 5.4 fusion.13
  324.4 96.9 %all-reduce.13.cloned.1.call-done = f32[2,320,32]{1,2,0:T(8,128)} async-done(((f32[2,320,32]{1,2,0:T(8,128)}), f32[2,320,32]{1,2,0:T(8,128)}) %all-reduce.13.cloned.1.call-update) | async-done | bytes 81936 | tf_op jit(solution)/shard_map/psum | solution.py:46
  421.3 1.2 fusion.14
  422.5 13.2 %psum.68 = f32[2,32,32]{1,2,0:T(8,128)S(1)} all-reduce(f32[2,32,32]{1,2,0:T(8,128)S(1)} %fusion.14), channel_id=1, replica_groups=mesh['replica'=32,'shard'=4] {'shard'}, use_global_device_ids=true, to_apply=%region_7.10 | all-reduce | flops 2048 | bytes 16384 | tf_op jit(solution)/shard_map/psum | solution.py:22
  435.9 5.9 custom-call.16
  442.0 4.9 custom-call.17
  446.9 1.2 convolution_bitcast_fusion
  448.1 4.6 fusion.15
  452.8 68.1 %psum.71 = f32[4,320]{1,0:T(4,128)S(1)} all-reduce(f32[4,320]{1,0:T(4,128)S(1)} %bitcast.57), channel_id=1, replica_groups=mesh['replica'=32,'shard'=4] {'replica'}, use_global_device_ids=true, to_apply=%region_10.13 | all-reduce | flops 1280 | bytes 10240 | tf_op jit(solution)/shard_map/psum | solution.py:41
  520.9 0.6 multiply_subtract_fusion.1
  521.6 96.2 %all-reduce.17.cloned.1.call-done = f32[2,1280,32]{1,2,0:T(8,128)} async-done(((f32[2,1280,32]{1,2,0:T(8,128)}), f32[2,1280,32]{1,2,0:T(8,128)}) %all-reduce.17.cloned.1.call-update) | async-done | bytes 327696 | tf_op jit(solution)/shard_map/psum | solution.py:32
  617.8 11.3 %multiply_subtract_fusion = (f32[2,320,1280]{2,1,0:T(8,128)}, f32[2,320,1280]{2,1,0:T(8,128)}, f32[1,2,320,1280]{3,2,1,0:T(8,128)}) fusion(f32[2,320,1280]{2,1,0:T(8,128)} %param.15, f32[2,320,1280]{2,1,0:T(8,128)} %param.16, f32[2,320,1280]{2,1,0:T(8,128)} %copy-done.1, f32[2,320,32]{1,2,0:T(8,128)S(1)} %convolution_bitcast_fusion, ...), kind=kOutput, calls=%fused_computation.3 | convolution fusion | flops 319488000 | bytes 20070400 | tf_op jit(solution)/shard_map/mdk,mek->mde/dot_general | solution.py:49
  (37 shorter events, 1.1 us)
Async XLA Ops:
  7.2 1.7 copy-start
  7.2 11.9 %copy-start.2 = (f32[2,1280,32]{1,2,0:T(8,128)S(1)}, f32[2,1280,32]{1,2,0:T(8,128)}, u32[]{:S(2)}) copy-start(f32[2,1280,32]{1,2,0:T(8,128)} %param.17) | copy-start | bytes 983044
  7.2 116.5 %all-reduce.7.cloned.1.call-start = ((), (), s32[]{:S(2)}) async-start(), calls=%async_computation | async-start | bytes 196608 | tf_op jit(solution)/shard_map/psum | solution.py:42
  17.4 1.7 copy-start.1
  22.7 173.9 %all-reduce.9.cloned.1.call-start = ((), (), s32[]{:S(2)}) async-start(), calls=%async_computation.1 | async-start | bytes 655360 | tf_op jit(solution)/shard_map/psum | solution.py:32
  155.1 149.7 %all-reduce.11.cloned.1.call-start = ((), (), s32[]{:S(2)}) async-start(), calls=%async_computation.2 | async-start | bytes 655360 | tf_op jit(solution)/shard_map/psum | solution.py:32
  196.6 224.7 %all-reduce.13.cloned.1.call-start = ((), (), s32[]{:S(2)}) async-start(), calls=%async_computation.3 | async-start | bytes 196608 | tf_op jit(solution)/shard_map/psum | solution.py:46
  324.3 128.5 %copy-start.3 = (f32[1,4,320]{2,1,0:T(4,128)S(1)}, f32[1,4,320]{2,1,0:T(4,128)}, u32[]{:S(2)}) copy-start(f32[1,4,320]{2,1,0:T(4,128)} %param.18) | copy-start | bytes 15364
  324.3 196.6 %copy-start.4 = (f32[4,320]{1,0:T(4,128)S(1)}, f32[4,320]{1,0:T(4,128)}, u32[]{:S(2)}) copy-start(f32[4,320]{1,0:T(4,128)} %param.19) | copy-start | bytes 15364
  324.3 196.6 %copy-start.5 = (f32[4,320]{1,0:T(4,128)S(1)}, f32[4,320]{1,0:T(4,128)}, u32[]{:S(2)}) copy-start(f32[4,320]{1,0:T(4,128)} %param.20) | copy-start | bytes 15364
  324.4 196.5 %all-reduce.15.cloned.1.call-start = ((), (), s32[]{:S(2)}) async-start(), calls=%async_computation.4 | async-start | bytes 655360 | tf_op jit(solution)/shard_map/psum | solution.py:32
  452.7 165.0 %all-reduce.17.cloned.1.call-start = ((), (), s32[]{:S(2)}) async-start(), calls=%async_computation.5 | async-start | bytes 655360 | tf_op jit(solution)/shard_map/psum | solution.py:32
Sparse Core Ops, SparseCore 0:
  22.8 100.8 all-reduce.6
  155.2 41.2 all-reduce.8
  200.2 104.5 all-reduce.10
  324.5 96.7 all-reduce.12
  452.9 41.2 all-reduce.14
  521.0 96.6 all-reduce.16

commit v2 on v0

--- a/solution.py
+++ b/solution.py
@@ -43,7 +43,7 @@
     left = orth_rows(left_sum)
     right = reduce_right(full, left)
     right_hat = orth_local(right)
-    left_sum = lax.psum(project_rows(full, right_hat), "replica")
+    left_sum = jnp.sum(lax.all_gather(project_rows(full, right_hat), "replica"), axis=0)
     left = orth_rows(left_sum)
     right = reduce_right(full, left)
     approx = jnp.einsum("mdk,mek->mde", left, right, precision=HIGH) / replicas

time: 610 us -> 577 us (0.946)
  waiting for transfers between devices: 423 us -> 390 us
    psum x1 -> x0, waiting for transfers between devices: 32.9 us -> none  [body(): left_sum = lax.psum(project_rows(full, right_hat), 'replica')]
  transfers between devices with their start and end apart: 4 -> 4, of which waited for: 4 -> 3; matrix products, arithmetic and copies ran while one was open for 0% -> 0% of each run, Pallas kernels for 0% -> 0%
where the time goes in v2:
time: 577 us
  waiting for transfers between devices  390 us (68%)
  blocking collectives  89.2 us (15%)
  matrix products  43.9 us (8%)
  other arithmetic  35.8 us (6%)
  between operations  13.9 us (2%)
    psum x2, waiting for transfers between devices, reduce_right(): return lax.psum(terms, ('replica', 'shard'))  289 us
    psum x1, waiting for transfers between devices, body(): left_sum = lax.psum(local_left, 'replica')  101 us
    psum x1, blocking collectives, body(): vec_total = lax.psum(vec_grads[0], 'replica')  62.9 us
    psum x2, blocking collectives, orth_rows(): gram = lax.psum(gram, 'shard')  26.3 us
    another operation x10, other arithmetic, finish(): lower = jnp.linalg.cholesky(gram)  18.1 us
    another operation x7, other arithmetic, finish(): lax.linalg.triangular_solve(lower, block, left_side=False, lower=True, tr...  15 us
  transfers between devices with their start and end apart: 4, of which 3 were waited for; matrix products, arithmetic and copies ran while one was open for 0% of the time, Pallas kernels for 0%

profile of v2, /device:TPU:1, one launch (start us, length us, event | category | flops | bytes accessed | tf_op | source)
XLA Modules:
  0.0 576.6 jit_solution(5966586106140662839)
XLA Ops:
  7.2 1.7 copy-done
  8.9 8.5 %fusion = f32[2,320,1280]{2,1,0:T(8,128)S(1)} fusion(bf16[2,2048,320]{1,2,0:T(8,128)(2,1)S(1)} %copy-done, bf16[2,2048,1280]{2,1,0:T(8,128)(2,1)} %param.13, f32[1,2,320,1280]{3,2,1,0:T(8,128)} %param.14), kind=kOutput, calls=%fused_computation.2 | convolution fusion | flops 3357081600 | bytes 19660800 | tf_op jit(solution)/shard_map/mtd,mte->mde/dot_general | solution.py:38
  17.4 1.7 copy-done.1
  19.1 3.5 fusion.9
  22.7 101.0 %all-reduce.4.cloned.1.call-done = f32[2,320,32]{1,2,0:T(8,128)} async-done(((f32[2,320,32]{1,2,0:T(8,128)}), f32[2,320,32]{1,2,0:T(8,128)}) %all-reduce.4.cloned.1.call-update) | async-done | bytes 81936 | tf_op jit(solution)/shard_map/psum | solution.py:42
  123.7 1.2 fusion.10
  124.9 13.2 %psum.43 = f32[2,32,32]{1,2,0:T(8,128)S(1)} all-reduce(f32[2,32,32]{1,2,0:T(8,128)S(1)} %fusion.10), channel_id=1, replica_groups=mesh['replica'=32,'shard'=4] {'shard'}, use_global_device_ids=true, to_apply=%region_1.0 | all-reduce | flops 2048 | bytes 16384 | tf_op jit(solution)/shard_map/psum | solution.py:22
  138.2 5.9 %custom-call.13 = f32[2,32,32]{2,1,0:T(8,128)S(1)} custom-call(f32[2,32,32]{2,1,0:T(8,128)S(1)} %fusion.7), custom_call_target="Cholesky" | custom-call | tf_op jit(solution)/shard_map/jit(cholesky)/cholesky | solution.py:11
  144.1 0.1 compare_reduce_fusion.2
  144.3 4.9 custom-call.14
  149.3 1.2 convolution_bitcast_fusion.1
  150.5 4.6 fusion.11
  155.1 0.2 all-gather.3.cloned.1.call-start
  155.4 144.9 %all-reduce.6.cloned.1.call-done = f32[2,1280,32]{1,2,0:T(8,128)} async-done(((f32[2,1280,32]{1,2,0:T(8,128)}), f32[2,1280,32]{1,2,0:T(8,128)}) %all-reduce.6.cloned.1.call-update) | async-done | bytes 327696 | tf_op jit(solution)/shard_map/psum | solution.py:32
  300.3 1.5 fusion.12
  301.9 5.9 %custom-call.15 = f32[2,32,32]{2,1,0:T(8,128)S(1)} custom-call(f32[2,32,32]{2,1,0:T(8,128)S(1)} %fusion.5), custom_call_target="Cholesky" | custom-call | tf_op jit(solution)/shard_map/jit(cholesky)/cholesky | solution.py:11
  307.8 0.1 compare_reduce_fusion.1
  308.0 4.9 custom-call.9
  312.9 1.5 fusion.3
  314.4 5.4 fusion.13
  319.9 62.9 %psum.47 = f32[4,320]{1,0:T(4,128)S(1)} all-reduce(f32[4,320]{1,0:T(4,128)S(1)} %bitcast.59), channel_id=1, replica_groups=mesh['replica'=32,'shard'=4] {'replica'}, use_global_device_ids=true, to_apply=%region_8.11 | all-reduce | flops 1280 | bytes 10240 | tf_op jit(solution)/shard_map/psum | solution.py:41
  382.8 2.1 reduce_sum.9
  384.9 0.2 fusion.14
  385.2 13.1 %psum.45 = f32[2,32,32]{1,2,0:T(8,128)S(1)} all-reduce(f32[2,32,32]{1,2,0:T(8,128)S(1)} %fusion.14), channel_id=1, replica_groups=mesh['replica'=32,'shard'=4] {'shard'}, use_global_device_ids=true, to_apply=%region_6.9 | all-reduce | flops 2048 | bytes 16384 | tf_op jit(solution)/shard_map/psum | solution.py:22
  398.4 5.9 %custom-call.16 = f32[2,32,32]{2,1,0:T(8,128)S(1)} custom-call(f32[2,32,32]{2,1,0:T(8,128)S(1)} %fusion.2), custom_call_target="Cholesky" | custom-call | tf_op jit(solution)/shard_map/jit(cholesky)/cholesky | solution.py:11
  404.3 0.1 compare_reduce_fusion
  404.5 4.9 custom-call.17
  409.4 0.3 convolution_bitcast_fusion
  409.7 4.6 fusion.15
  414.4 0.6 multiply_subtract_fusion.1
  415.0 143.9 %all-reduce.8.cloned.1.call-done = f32[2,1280,32]{1,2,0:T(8,128)} async-done(((f32[2,1280,32]{1,2,0:T(8,128)}), f32[2,1280,32]{1,2,0:T(8,128)}) %all-reduce.8.cloned.1.call-update) | async-done | bytes 327696 | tf_op jit(solution)/shard_map/psum | solution.py:32
  558.8 11.3 %multiply_subtract_fusion = (f32[2,320,1280]{2,1,0:T(8,128)}, f32[2,320,1280]{2,1,0:T(8,128)}, f32[1,2,320,1280]{3,2,1,0:T(8,128)}) fusion(f32[2,320,1280]{2,1,0:T(8,128)} %param.15, f32[2,320,1280]{2,1,0:T(8,128)} %param.16, f32[2,320,1280]{2,1,0:T(8,128)} %copy-done.1, f32[2,320,32]{1,2,0:T(8,128)S(1)} %convolution_bitcast_fusion, ...), kind=kOutput, calls=%fused_computation.3 | convolution fusion | flops 319488000 | bytes 20070400 | tf_op jit(solution)/shard_map/mdk,mek->mde/dot_general | solution.py:49
  (32 shorter events, 0.8 us)
Async XLA Ops:
  7.2 1.7 copy-start
  7.2 11.9 %copy-start.2 = (f32[2,1280,32]{1,2,0:T(8,128)S(1)}, f32[2,1280,32]{1,2,0:T(8,128)}, u32[]{:S(2)}) copy-start(f32[2,1280,32]{1,2,0:T(8,128)} %param.17) | copy-start | bytes 983044
  7.2 116.5 %all-reduce.4.cloned.1.call-start = ((), (), s32[]{:S(2)}) async-start(), calls=%async_computation | async-start | bytes 196608 | tf_op jit(solution)/shard_map/psum | solution.py:42
  17.4 1.7 copy-start.1
  22.7 277.6 %all-reduce.6.cloned.1.call-start = ((), (), s32[]{:S(2)}) async-start(), calls=%async_computation.1 | async-start | bytes 655360 | tf_op jit(solution)/shard_map/psum | solution.py:32
  155.1 164.8 %copy-start.3 = (f32[1,4,320]{2,1,0:T(4,128)S(1)}, f32[1,4,320]{2,1,0:T(4,128)}, u32[]{:S(2)}) copy-start(f32[1,4,320]{2,1,0:T(4,128)} %param.18) | copy-start | bytes 15364
  155.1 227.7 %all-gather.3.cloned.1.call-start = ((), (), s32[]{:S(2)}) async-start(), calls=%async_computation.3 | async-start | bytes 3244032 | tf_op jit(solution)/shard_map/all_gather | solution.py:46
  319.8 239.0 %all-reduce.8.cloned.1.call-start = ((), (), s32[]{:S(2)}) async-start(), calls=%async_computation.2 | async-start | bytes 655360 | tf_op jit(solution)/shard_map/psum | solution.py:32
  382.8 31.6 %copy-start.4 = (f32[4,320]{1,0:T(4,128)S(1)}, f32[4,320]{1,0:T(4,128)}, u32[]{:S(2)}) copy-start(f32[4,320]{1,0:T(4,128)} %param.19) | copy-start | bytes 15364
  382.8 31.6 %copy-start.5 = (f32[4,320]{1,0:T(4,128)S(1)}, f32[4,320]{1,0:T(4,128)}, u32[]{:S(2)}) copy-start(f32[4,320]{1,0:T(4,128)} %param.20) | copy-start | bytes 15364
Sparse Core Ops, SparseCore 0:
  22.8 100.8 all-reduce.3
  155.2 144.9 all-reduce.5
  319.9 43.4 all-gather.2
  414.5 144.3 all-reduce.7
